TPU v7x, 32 devices: a whole 2x2x4 slice. The times are simulated.
32 devices in a mesh: groups: 2 (over y), tm: 4 (over x, core), tensor: 4 (over z).
Axes of the slice: x: 2, y: 2, z: 4, core: 2. Of those that a mesh axis runs over, the one named last changes fastest.
Arguments:
- start_latent: float32 [256, 128], P(('groups', 'tensor')), parts along dimension 0, may hold values from -6 to 6
- time_index: int32 [8], P(('groups', 'tm')), parts along dimension 0, may hold values from 39 to 998, as said below
- step_weight: int32 [8], P(('groups', 'tm')), parts along dimension 0, may hold values from 1 to 16
- in_weight: bfloat16 [128, 3072], P('tm'), may hold values from -0.5 to 0.5
- mod_weight: bfloat16 [256, 9216], P(None, 'tensor'), may hold values from -0.375 to 0.375
- qkv_weight: bfloat16 [3072, 6144], P(None, 'tensor'), as said below
- out_weight: bfloat16 [2048, 3072], P('tensor'), may hold values from -0.125 to 0.125
- head_weight: bfloat16 [3072, 128], P('tm'), may hold values from -0.109375 to 0.109375
Outputs:
- window_latents: float32 [8, 128, 128], P(('groups', 'tm'), 'tensor'), parts along dimension 0
There are 2 independent parts, one for each index of `groups`. A program takes and returns all parts, laid end to end along the dimension named above; an argument that names none is the same for every part. Nothing has to cross between parts.
Inputs may be any that keep to these rules, and one draw needn't show every extreme that they name: `time_index`: strictly decreasing indices of a 1000-step plan. `qkv_weight`: entries at most 24 / sqrt(3072) in magnitude.
All inputs are finite; a program needn't handle non-finite values.
Results may differ from a plain program's by a relative error of at most 0.0075.
Values may be sent and summed in bfloat16 or wider, within the bound.
A program may use at most 64 MiB of HBM per device.

v0:
```python
import math

import jax
import jax.numpy as jnp
from jax import lax
from jax.sharding import PartitionSpec as P

D = 3072
HD = 128
ITERS = 2


NORM_EPS = 1e-06
STEP_DIVISOR = 64.0


def carried_in(value, axis, combine, identity):
    devices, index = (lax.axis_size(axis), lax.axis_index(axis))
    everything = lax.all_gather(value, axis)
    start = jnp.broadcast_to(jnp.asarray(identity, value.dtype), value.shape)

    def turn(k, before):
        reached = k < index
        new = combine(before, everything[k])
        return jnp.where(reached, new, before)

    return lax.fori_loop(0, devices, turn, start)


def embedding_of(time_index, width):
    half_width = width // 2
    frequency = jnp.exp(
        -math.log(10000.0) * jnp.arange(half_width).astype(jnp.float32) / half_width
    )
    angles = time_index.astype(jnp.float32)[:, None] * frequency[None, :]
    return jnp.concatenate([jnp.cos(angles), jnp.sin(angles)], axis=1)


def attention(qkv_rows, head_count):
    token_count = qkv_rows.shape[0]
    packed = qkv_rows.reshape(token_count, head_count, 3, HD)
    queries = packed[:, :, 0]
    key_rows = packed[:, :, 1]
    values = packed[:, :, 2]
    block_rows = min(token_count, 512)

    def one_block(block_start):
        scores = jnp.einsum(
            "qhe,khe->hqk", queries, key_rows, preferred_element_type=jnp.float32
        ) * (1.0 / math.sqrt(HD))
        attention_weights = jax.nn.softmax(scores, axis=-1).astype(jnp.bfloat16)
        return jnp.einsum(
            "hqk,khe->qhe", attention_weights, values, preferred_element_type=jnp.float32
        ).astype(jnp.bfloat16)

    block_starts = jnp.arange(token_count // block_rows, dtype=jnp.int32) * block_rows
    blocks_out = lax.map(one_block, block_starts)
    return blocks_out.reshape(token_count, head_count * HD)


def evaluate(latents, shifts, scales, folded, in_weight_all, qkv_weight, head_count):
    widened = jnp.dot(latents, in_weight_all, preferred_element_type=jnp.float32)
    row_mean = jnp.mean(widened, axis=1, keepdims=True)
    centered = widened - row_mean
    spread = jnp.mean(centered * centered, axis=1, keepdims=True)
    normed = (centered * lax.rsqrt(spread + NORM_EPS) * (1.0 + scales) + shifts).astype(
        jnp.bfloat16
    )
    qkv_rows = jnp.dot(normed, qkv_weight, preferred_element_type=jnp.float32).astype(jnp.bfloat16)
    attended = attention(qkv_rows, head_count)
    return (widened, jnp.dot(attended, folded, preferred_element_type=jnp.float32))


def fold_head(out_weight, gate_rows, head_weight_all):
    scaled_out = (out_weight.astype(jnp.float32) * gate_rows[None, :]).astype(jnp.bfloat16)
    return jnp.dot(scaled_out, head_weight_all, preferred_element_type=jnp.float32).astype(
        jnp.bfloat16
    )


def add_terms(earlier, later):
    return earlier + later


def local(
    start_latent,
    time_index,
    step_weight,
    in_weight,
    mod_weight,
    qkv_weight,
    out_weight,
    head_weight,
):
    rows_dev = start_latent.shape[0]
    head_count = qkv_weight.shape[1] // (3 * HD)
    in_weight_all, head_weight_all = (
        lax.all_gather(in_weight, "tm", axis=0, tiled=True),
        lax.all_gather(head_weight, "tm", axis=0, tiled=True),
    )
    embedding = embedding_of(time_index, mod_weight.shape[0]).astype(jnp.bfloat16)
    mod_part = jnp.dot(embedding, mod_weight, preferred_element_type=jnp.float32)
    modulation = lax.all_gather(mod_part, "tensor", axis=1, tiled=True)
    shifts = modulation[:, :D]
    scales = modulation[:, D : 2 * D]
    gate_rows = modulation[:, 2 * D :]
    folded = fold_head(out_weight, gate_rows[0], head_weight_all)
    step_size = step_weight.astype(jnp.float32) / STEP_DIVISOR
    start_all = lax.all_gather(start_latent, "tensor", axis=0, tiled=True)
    row_first = lax.axis_index("tensor") * rows_dev
    guesses = start_all.astype(jnp.bfloat16)[None]
    window_end = start_latent[None]
    for iteration in range(ITERS):
        widened, partial_sum = evaluate(
            guesses[0], shifts[0], scales[0], folded, in_weight_all, qkv_weight, head_count
        )
        widened_list = [widened]
        partials = [partial_sum]
        stacked = jnp.stack(partials, 0)
        residual = jnp.stack(
            [
                jnp.dot(
                    lax.dynamic_slice_in_dim(widened, row_first, rows_dev, 0).astype(jnp.bfloat16),
                    head_weight_all,
                    preferred_element_type=jnp.float32,
                )
                for widened in widened_list
            ],
            0,
        )
        velocity = lax.psum_scatter(stacked, "tensor", scatter_dimension=1, tiled=True) + residual
        drifts = step_size[:, None, None] * velocity
        inclusive = jnp.cumsum(drifts, axis=0)
        earlier = carried_in(inclusive[-1], "tm", add_terms, jnp.zeros_like(inclusive[-1]))
        window_end = start_latent[None] + earlier[None] + inclusive
        if iteration + 1 < ITERS:
            guesses = lax.all_gather(
                (window_end - drifts).astype(jnp.bfloat16), "tensor", axis=1, tiled=True
            )
    return window_end


def solution(mesh):
    return jax.shard_map(
        local,
        mesh=mesh,
        in_specs=(
            P(("groups", "tensor"), None),
            P(("groups", "tm")),
            P(("groups", "tm")),
            P("tm", None),
            P(None, "tensor"),
            P(None, "tensor"),
            P("tensor", None),
            P("tm", None),
        ),
        out_specs=P(("groups", "tm"), "tensor", None),
        check_vma=False,
    )
```

profile of v0, /device:TPU:0, one launch (start us, length us, event | category | flops | bytes accessed | tf_op | source)
XLA Modules:
  0.0 162.6 jit_solution(14899555492809119197)
XLA Ops:
  6.5 10.4 %all_gather.22 = bf16[128,3072]{1,0:T(8,128)(2,1)S(1)} all-gather(bf16[32,3072]{1,0:T(8,128)(2,1)} %param.15), channel_id=1, replica_groups=mesh['groups'=2,'tm'=4,'tensor'=4] {'tm'}, dimensions={0}, use_global_device_ids=true | all-gather | bytes 983040 | tf_op jit(solution)/shard_map/all_gather | solution.py:98
  16.9 0.7 convert.14
  17.7 13.4 %all_gather.21 = bf16[128,128]{1,0:T(8,128)(2,1)S(1)} all-gather(bf16[32,128]{1,0:T(8,128)(2,1)S(1)} %convert.14), channel_id=1, replica_groups=mesh['groups'=2,'tm'=4,'tensor'=4] {'tensor'}, dimensions={0}, use_global_device_ids=true | all-gather | bytes 40960 | tf_op jit(solution)/shard_map/all_gather | solution.py:109
  32.8 13.2 %all-gather.1 = f32[4,1,2304]{2,1,0:T(1,128)S(1)} all-gather(f32[1,1,2304]{2,1,0:T(1,128)S(1)} %convolution_bitcast_fusion), channel_id=2, replica_groups=mesh['groups'=2,'tm'=4,'tensor'=4] {'tensor'}, dimensions={0}, use_global_device_ids=true | all-gather | bytes 46080 | tf_op jit(solution)/shard_map/all_gather | solution.py:103
  46.0 0.6 copy-done.3
  46.6 5.9 %convolution_convert_fusion.1 = bf16[128,1536]{1,0:T(8,128)(2,1)} fusion(bf16[3072,1536]{1,0:T(8,128)(2,1)} %param.17, f32[128,3072]{1,0:T(8,128)S(1)} %get-tuple-element.245, f32[3072]{0:T(1024)S(1)} %bitcast.113, f32[3072]{0:T(1024)S(1)} %bitcast.115, f32[128]{0:T(128)S(1)} %add_rsqrt_fusion.1, f32[128]{0:T(128)S(1)} %broadcast_multiply_fusion.1), kind=kOutput, calls=%fused_computation.9 | convolution fusion | flops 1210122240 | bytes 11428864 | tf_op jit(solution)/shard_map/dot_general | solution.py:69
  52.5 1.9 %copy.27 = bf16[128,1536]{0,1:T(8,128)(2,1)} copy(bf16[128,1536]{1,0:T(8,128)(2,1)} %convolution_convert_fusion.1) | data formatting | bytes 786432 | tf_op jit(solution)/shard_map/convert_element_type | solution.py:69
  54.4 1.9 %convolution_multiply_fusion.1 = f32[4,128,128]{1,2,0:T(8,128)} fusion(bf16[128,4,3,128]{0,3,2,1:T(8,128)(2,1)} %bitcast.107), kind=kOutput, calls=%fused_computation.17 | convolution fusion | flops 16842752 | bytes 524288 | tf_op jit(solution)/shard_map/while/body/eval_jaxpr/qhe,khe->hqk/dot_general | solution.py:48
  56.3 1.3 fusion.36
  57.6 8.4 %all_gather.24 = bf16[3072,128]{1,0:T(8,128)(2,1)S(1)} all-gather(bf16[768,128]{1,0:T(8,128)(2,1)} %param.19), channel_id=1, replica_groups=mesh['groups'=2,'tm'=4,'tensor'=4] {'tm'}, dimensions={0}, use_global_device_ids=true | all-gather | bytes 983040 | tf_op jit(solution)/shard_map/all_gather | solution.py:99
  66.0 2.0 %convolution_convert_fusion.3 = bf16[4,128,128]{2,1,0:T(8,128)(2,1)} fusion(bf16[128,4,3,128]{0,3,2,1:T(8,128)(2,1)} %bitcast.109, f32[4,128]{1,0:T(4,128)S(1)} %fusion.36, f32[4,128,128]{1,2,0:T(8,128)} %convolution_multiply_fusion.1), kind=kOutput, calls=%fused_computation.21 | convolution fusion | flops 17040000 | bytes 788480 | tf_op jit(solution)/shard_map/while/body/eval_jaxpr/hqk,khe->qhe/dot_general | solution.py:52
  68.0 2.9 %fusion.8 = bf16[512,128]{1,0:T(8,128)(2,1)S(1)} fusion(bf16[3072,128]{1,0:T(8,128)(2,1)S(1)} %all_gather.24, bf16[512,3072]{1,0:T(8,128)(2,1)} %param.18, f32[3072]{0:T(1024)S(1)} %bitcast.120), kind=kOutput, calls=%fused_computation.22 | convolution fusion | flops 407437312 | bytes 4075520 | tf_op jit(solution)/shard_map/dot_general | solution.py:76
  70.9 0.6 copy-done.2
  71.6 0.8 convolution_bitcast_fusion.2
  73.2 19.2 %reduce-scatter.3.cloned.1.call-done = f32[1,32,128]{2,1,0:T(8,128)} async-done(((f32[1,128,128]{2,1,0:T(8,128)}), f32[1,32,128]{2,1,0:T(8,128)}) %reduce-scatter.3.cloned.1.call-update) | async-done | bytes 16400 | tf_op jit(solution)/shard_map/reduce_scatter | solution.py:131
  92.4 1.0 fusion.12
  93.3 0.6 copy-done.7
  93.9 5.2 %all_gather.25 = f32[4,32,128]{2,1,0:T(8,128)S(1)} all-gather(f32[1,32,128]{2,1,0:T(8,128)S(1)} %fusion.12), channel_id=1, replica_groups=mesh['groups'=2,'tm'=4,'tensor'=4] {'tm'}, dimensions={0}, use_global_device_ids=true | all-gather | bytes 81920 | tf_op jit(solution)/shard_map/all_gather | solution.py:19
  99.3 0.7 fusion.27
  100.0 13.1 %all_gather.26 = bf16[1,128,128]{2,1,0:T(8,128)(2,1)S(1)} all-gather(bf16[1,32,128]{2,1,0:T(8,128)(2,1)S(1)} %fusion.27), channel_id=1, replica_groups=mesh['groups'=2,'tm'=4,'tensor'=4] {'tensor'}, dimensions={1}, use_global_device_ids=true | all-gather | bytes 40960 | tf_op jit(solution)/shard_map/all_gather | solution.py:137
  113.1 1.6 fusion.37
  115.1 5.9 %convolution_convert_fusion = bf16[128,1536]{1,0:T(8,128)(2,1)} fusion(bf16[3072,1536]{1,0:T(8,128)(2,1)} %param.17, f32[128,3072]{1,0:T(8,128)S(1)} %get-tuple-element.247, f32[128]{0:T(128)S(1)} %add_rsqrt_fusion, f32[128]{0:T(128)S(1)} %broadcast_multiply_fusion, f32[3072]{0:T(1024)S(1)} %bitcast.114, f32[3072]{0:T(1024)S(1)} %bitcast.116), kind=kOutput, calls=%fused_computation.8 | convolution fusion | flops 1210122240 | bytes 11428864 | tf_op jit(solution)/shard_map/dot_general | solution.py:69
  121.0 1.9 %copy.32 = bf16[128,1536]{0,1:T(8,128)(2,1)} copy(bf16[128,1536]{1,0:T(8,128)(2,1)} %convolution_convert_fusion) | data formatting | bytes 786432 | tf_op jit(solution)/shard_map/convert_element_type | solution.py:69
  122.9 1.9 %convolution_multiply_fusion = f32[4,128,128]{1,2,0:T(8,128)} fusion(bf16[128,4,3,128]{0,3,2,1:T(8,128)(2,1)} %bitcast.110), kind=kOutput, calls=%fused_computation.16 | convolution fusion | flops 16842752 | bytes 524288 | tf_op jit(solution)/shard_map/while/body/eval_jaxpr/qhe,khe->hqk/dot_general | solution.py:48
  124.8 1.3 fusion.38
  126.1 2.0 %convolution_convert_fusion.2 = bf16[4,128,128]{2,1,0:T(8,128)(2,1)} fusion(bf16[128,4,3,128]{0,3,2,1:T(8,128)(2,1)} %bitcast.112, f32[4,128]{1,0:T(4,128)S(1)} %fusion.38, f32[4,128,128]{1,2,0:T(8,128)} %convolution_multiply_fusion), kind=kOutput, calls=%fused_computation.20 | convolution fusion | flops 17040000 | bytes 788480 | tf_op jit(solution)/shard_map/while/body/eval_jaxpr/hqk,khe->qhe/dot_general | solution.py:52
  128.0 1.8 %convolution_bitcast_fusion.1 = f32[1,128,128]{2,1,0:T(8,128)} fusion(bf16[128,512]{0,1:T(8,128)(2,1)} %bitcast.119, bf16[512,128]{1,0:T(8,128)(2,1)} %copy-done.2), kind=kOutput, calls=%fused_computation.23 | convolution fusion | flops 16777216 | bytes 327680 | tf_op jit(solution)/shard_map/dot_general | solution.py:71
  129.9 17.6 %reduce-scatter.5.cloned.1.call-done = f32[1,32,128]{2,1,0:T(8,128)} async-done(((f32[1,128,128]{2,1,0:T(8,128)}), f32[1,32,128]{2,1,0:T(8,128)}) %reduce-scatter.5.cloned.1.call-update) | async-done | bytes 16400 | tf_op jit(solution)/shard_map/reduce_scatter | solution.py:131
  147.5 1.0 fusion.10
  148.5 0.6 copy-done.8
  149.1 5.2 %all_gather.27 = f32[4,32,128]{2,1,0:T(8,128)S(1)} all-gather(f32[1,32,128]{2,1,0:T(8,128)S(1)} %fusion.10), channel_id=1, replica_groups=mesh['groups'=2,'tm'=4,'tensor'=4] {'tm'}, dimensions={0}, use_global_device_ids=true | all-gather | bytes 81920 | tf_op jit(solution)/shard_map/all_gather | solution.py:19
  154.4 1.3 bitcast_add_fusion
  (44 shorter events, 1.8 us)
Async XLA Ops:
  6.5 26.0 %copy-start = (bf16[256,2304]{1,0:T(8,128)(2,1)S(1)}, bf16[256,2304]{1,0:T(8,128)(2,1)}, u32[]{:S(2)}) copy-start(bf16[256,2304]{1,0:T(8,128)(2,1)} %param.16) | copy-start | bytes 3538948
  6.5 85.8 %reduce-scatter.3.cloned.1.call-start = ((), (), s32[]{:S(2)}) async-start(), calls=%async_computation.2 | async-start | bytes 81920 | tf_op jit(solution)/shard_map/reduce_scatter | solution.py:131
  16.9 35.6 %copy-start.1 = (bf16[128,3072]{1,0:T(8,128)(2,1)}, bf16[128,3072]{1,0:T(8,128)(2,1)S(1)}, u32[]{:S(2)}) copy-start(bf16[128,3072]{1,0:T(8,128)(2,1)S(1)} %all_gather.22) | copy-start | bytes 2359300
  46.0 0.6 copy-start.3
  46.0 0.6 copy-start.5
  68.0 3.6 %copy-start.9 = (bf16[4,128,128]{2,1,0:T(8,128)(2,1)S(1)}, bf16[4,128,128]{2,1,0:T(8,128)(2,1)}, u32[]{:S(2)}) copy-start(bf16[4,128,128]{2,1,0:T(8,128)(2,1)} %convolution_convert_fusion.3) | copy-start | bytes 393220
  70.9 0.7 copy-start.2
  72.4 75.1 %reduce-scatter.5.cloned.1.call-start = ((), (), s32[]{:S(2)}) async-start(), calls=%async_computation.3 | async-start | bytes 81920 | tf_op jit(solution)/shard_map/reduce_scatter | solution.py:131
  93.3 0.6 copy-start.7
  113.1 1.9 %copy-start.4 = (f32[1,3072]{1,0:T(1,128)S(1)}, f32[1,3072]{1,0:T(1,128)}, u32[]{:S(2)}) copy-start(f32[1,3072]{1,0:T(1,128)} %copy-done.3) | copy-start | bytes 36868
  113.1 1.9 %copy-start.6 = (f32[1,3072]{1,0:T(1,128)S(1)}, f32[1,3072]{1,0:T(1,128)}, u32[]{:S(2)}) copy-start(f32[1,3072]{1,0:T(1,128)} %copy-done.5) | copy-start | bytes 36868
  148.5 0.6 copy-start.8
Sparse Core Ops, SparseCore 0:
  72.6 19.7 reduce-scatter.2
  130.0 17.4 reduce-scatter.4
where the time goes:
time: 163 us
  blocking collectives  68.9 us (42%)
  waiting for transfers between devices  36.8 us (23%)
  matrix products  31.9 us (20%)
  between operations  14.9 us (9%)
  local copies, waits for them, and re-layouts  6.27 us (4%)
  other arithmetic  3.61 us (2%)
    reduce_scatter x2, waiting for transfers between devices, local(): lax.psum_scatter(stacked, 'tensor', scatter_dimension=1, tiled=True)  36.8 us
    all_gather x1, blocking collectives, local(): start_all = lax.all_gather(start_latent, 'tensor', axis=0, tiled=True)  13.4 us
    all_gather x1, blocking collectives, local(): modulation = lax.all_gather(mod_part, 'tensor', axis=1, tiled=True)  13.2 us
    all_gather x1, blocking collectives, local(): lax.all_gather((window_end - drifts).astype(jnp.bfloat16), 'tensor', axis...  13.1 us
    dot_general x2, matrix products, evaluate(): jnp.dot(normed, qkv_weight, preferred_element_type=jnp.float32)  11.8 us
    all_gather x2, blocking collectives, carried_in(): everything = lax.all_gather(value, axis)  10.4 us
    all_gather x1, blocking collectives, local(): lax.all_gather(in_weight, 'tm', axis=0, tiled=True)  10.4 us
    all_gather x1, blocking collectives, local(): lax.all_gather(head_weight, 'tm', axis=0, tiled=True)  8.41 us
  transfers between devices with their start and end apart: 2, of which 2 were waited for; matrix products, arithmetic and copies ran while one was open for 0% of the time, Pallas kernels for 0%

commit v1 on v0

--- a/solution.py
+++ b/solution.py
@@ -3,6 +3,8 @@
 import jax
 import jax.numpy as jnp
 from jax import lax
+from jax.experimental import pallas as pl
+from jax.experimental.pallas import tpu as pltpu
 from jax.sharding import PartitionSpec as P
 
 D = 3072
@@ -140,9 +142,409 @@
     return window_end
 
 
+MESH = pl.DeviceIdType.MESH
+
+
+def fused_kernel(
+    tm_size,
+    tensor_size,
+    start_ref,
+    time_ref,
+    step_ref,
+    in_ref,
+    mod_ref,
+    qkv_ref,
+    out_w_ref,
+    head_ref,
+    o_ref,
+    mod_v,
+    qkv_v,
+    out_v,
+    in_v,
+    head_v,
+    mods,
+    centered_v,
+    scaled_v,
+    table_v,
+    shift_v,
+    folded_v,
+    guess_v,
+    own_v,
+    part_v,
+    landed_v,
+    drift_v,
+    drifts_v,
+    local_sem,
+    in_send,
+    in_recv,
+    head_send,
+    head_recv,
+    mod_send,
+    mod_recv,
+    guess_send,
+    guess_recv,
+    part_send,
+    part_recv,
+    drift_send,
+    drift_recv,
+):
+    me = lax.axis_index("tm")
+    mine = lax.axis_index("tensor")
+    chips = tm_size // 2
+    chip, core = me // 2, lax.rem(me, 2)
+    partner = chip * 2 + (1 - core)
+    rows = start_ref.shape[0]
+    channels = start_ref.shape[1]
+    in_rows = in_ref.shape[0]
+    head_rows = head_ref.shape[0]
+    heads = qkv_ref.shape[1] // (3 * HD)
+
+    barrier = pltpu.get_barrier_semaphore()
+    for k in range(1, tm_size):
+        pl.semaphore_signal(
+            barrier, inc=1, device_id={"tm": lax.rem(me + k, tm_size)}, device_id_type=MESH
+        )
+    for k in range(1, tensor_size):
+        pl.semaphore_signal(
+            barrier,
+            inc=1,
+            device_id={"tensor": lax.rem(mine + k, tensor_size)},
+            device_id_type=MESH,
+        )
+
+    def row_block(ref, index, count):
+        return ref.at[pl.ds(pl.multiple_of(index * count, count), count)]
+
+    copy_mod = pltpu.make_async_copy(mod_ref, mod_v, local_sem.at[0])
+    copy_in = pltpu.make_async_copy(in_ref, row_block(in_v, me, in_rows), local_sem.at[1])
+    copy_head = pltpu.make_async_copy(head_ref, row_block(head_v, me, head_rows), local_sem.at[2])
+    copy_out = pltpu.make_async_copy(out_w_ref, out_v, local_sem.at[3])
+    copy_qkv = pltpu.make_async_copy(qkv_ref, qkv_v, local_sem.at[4])
+    for copy in (copy_mod, copy_in, copy_head, copy_out, copy_qkv):
+        copy.start()
+    pl.semaphore_wait(barrier, tm_size - 1 + tensor_size - 1)
+
+    def to_tm(src, dst, send, recv, target):
+        return pltpu.make_async_remote_copy(
+            src_ref=src,
+            dst_ref=dst,
+            send_sem=send,
+            recv_sem=recv,
+            device_id={"tm": target},
+            device_id_type=MESH,
+        )
+
+    def to_tensor(src, dst, send, recv, target):
+        return pltpu.make_async_remote_copy(
+            src_ref=src,
+            dst_ref=dst,
+            send_sem=send,
+            recv_sem=recv,
+            device_id={"tensor": target},
+            device_id_type=MESH,
+        )
+
+    def start_gather(source, full, count, send, recv):
+        started = []
+        for k in range(1, chips):
+            target = lax.rem(chip + k, chips) * 2 + core
+            started.append(
+                to_tm(source, row_block(full, me, count), send.at[k], recv.at[k], target)
+            )
+        started.append(
+            to_tm(source, row_block(full, me, count), send.at[0], recv.at[0], partner)
+        )
+        for copy in started:
+            copy.start()
+        return started
+
+    def relay_gather(full, count, send, recv):
+        started = []
+        for k in range(1, chips):
+            source = lax.rem(chip + chips - k, chips) * 2 + core
+            block = row_block(full, source, count)
+            to_tm(block, block, send.at[k], recv.at[k], partner).wait_recv()
+            relay = to_tm(block, block, send.at[chips + k], recv.at[chips + k], partner)
+            relay.start()
+            started.append(relay)
+        return started
+
+    def end_gather(full, count, send, recv):
+        block = row_block(full, partner, count)
+        to_tm(block, block, send.at[0], recv.at[0], partner).wait_recv()
+        for k in range(1, chips):
+            source = lax.rem(chip + chips - k, chips) * 2 + (1 - core)
+            block = row_block(full, source, count)
+            to_tm(block, block, send.at[k], recv.at[chips + k], partner).wait_recv()
+
+    def share(buffer, send, recv):
+        started = []
+        for k in range(1, tensor_size):
+            block = buffer.at[mine]
+            copy = to_tensor(
+                block, block, send.at[k], recv.at[k], lax.rem(mine + k, tensor_size)
+            )
+            copy.start()
+            started.append(copy)
+        return started
+
+    def shared(buffer, send, recv):
+        for k in range(1, tensor_size):
+            block = buffer.at[lax.rem(mine + tensor_size - k, tensor_size)]
+            to_tensor(block, block, send.at[k], recv.at[k], mine).wait_recv()
+
+    sends = []
+    sends += start_gather(in_ref, in_v, in_rows, in_send, in_recv)
+    sends += start_gather(head_ref, head_v, head_rows, head_send, head_recv)
+
+    start_own = start_ref[...]
+    own_v[...] = start_own.astype(jnp.bfloat16)
+    guess_v[0, mine] = start_own.astype(jnp.bfloat16)
+    sends += share(guess_v.at[0], guess_send.at[0], guess_recv.at[0])
+
+    half = mod_ref.shape[0] // 2
+    order = lax.broadcasted_iota(jnp.int32, (8, half), 1).astype(jnp.float32)
+    frequency = jnp.exp(-math.log(10000.0) * order / half)
+    angles = time_ref[0].astype(jnp.float32) * frequency
+    embedding = jnp.concatenate([jnp.cos(angles), jnp.sin(angles)], axis=1).astype(jnp.bfloat16)
+    copy_mod.wait()
+    mod_part = jnp.dot(embedding, mod_v[...], preferred_element_type=jnp.float32)
+    mods[mine] = mod_part[0:1]
+    sends += share(mods, mod_send, mod_recv)
+
+    copy_in.wait()
+    sends += relay_gather(in_v, in_rows, in_send, in_recv)
+    shared(mods, mod_send, mod_recv)
+    modulation = jnp.concatenate([mods[k] for k in range(tensor_size)], axis=1)
+    shifts = modulation[:, :D]
+    scales = 1.0 + modulation[:, D : 2 * D]
+    gates = modulation[:, 2 * D :]
+    copy_out.wait()
+    step_rows = 128
+    for r in range(0, out_v.shape[0], step_rows):
+        out_v[r : r + step_rows] = (
+            out_v[r : r + step_rows].astype(jnp.float32) * gates
+        ).astype(jnp.bfloat16)
+
+    high = shifts.astype(jnp.bfloat16)
+    low = (shifts - high.astype(jnp.float32)).astype(jnp.bfloat16)
+    row_id = lax.broadcasted_iota(jnp.int32, (16, D), 0)
+    pair = jnp.where(
+        row_id == 0,
+        high.astype(jnp.float32),
+        jnp.where(row_id == 1, low.astype(jnp.float32), 0.0),
+    )
+    scaled_v[channels : channels + 16] = pair.astype(jnp.bfloat16)
+
+    end_gather(in_v, in_rows, in_send, in_recv)
+    for r in range(0, channels, 32):
+        block = in_v[r : r + 32].astype(jnp.float32)
+        block = block - jnp.mean(block, axis=1, keepdims=True)
+        centered_v[r : r + 32] = block.astype(jnp.bfloat16)
+        scaled_v[r : r + 32] = (block * scales).astype(jnp.bfloat16)
+
+    copy_qkv.wait()
+    for h in range(heads):
+        columns = slice(3 * HD * h, 3 * HD * (h + 1))
+        product = jnp.dot(
+            scaled_v[...], qkv_v[:, columns], preferred_element_type=jnp.float32
+        )
+        main = product[:channels]
+        main_high = main.astype(jnp.bfloat16)
+        table_v[:channels, columns] = main_high
+        table_v[channels:, columns] = (main - main_high.astype(jnp.float32)).astype(jnp.bfloat16)
+        shift_v[:, columns] = product[channels : channels + 1] + product[channels + 1 : channels + 2]
+    centered = centered_v[...]
+    spread_table = lax.dot_general(
+        centered, centered, (((1,), (1,)), ((), ())), preferred_element_type=jnp.float32
+    ) * (1.0 / D)
+    spread_high = spread_table.astype(jnp.bfloat16)
+    spread_low = (spread_table - spread_high.astype(jnp.float32)).astype(jnp.bfloat16)
+    spread_pair = jnp.concatenate([spread_high, spread_low], axis=0)
+
+    sends += relay_gather(head_v, head_rows, head_send, head_recv)
+    copy_head.wait()
+    shared(guess_v.at[0], guess_send.at[0], guess_recv.at[0])
+
+    step_size = step_ref[0].astype(jnp.float32) / STEP_DIVISOR
+    residual_pair = None
+    for iteration in range(ITERS):
+        guess = jnp.concatenate([guess_v[iteration, k] for k in range(tensor_size)], axis=0)
+        twice = jnp.concatenate([guess, guess], axis=1)
+        spread = jnp.sum(
+            jnp.dot(twice, spread_pair, preferred_element_type=jnp.float32)
+            * guess.astype(jnp.float32),
+            axis=1,
+            keepdims=True,
+        )
+        inverse = lax.rsqrt(jnp.maximum(spread, 0.0) + NORM_EPS)
+        qkv_rows = jnp.dot(twice, table_v[...], preferred_element_type=jnp.float32)
+        qkv_rows = (qkv_rows * inverse + shift_v[...]).astype(jnp.bfloat16)
+        attended = []
+        for h in range(heads):
+            first = 3 * HD * h
+            query = qkv_rows[:, first : first + HD]
+            key = qkv_rows[:, first + HD : first + 2 * HD]
+            value = qkv_rows[:, first + 2 * HD : first + 3 * HD]
+            scores = lax.dot_general(
+                query, key, (((1,), (1,)), ((), ())), preferred_element_type=jnp.float32
+            ) * (1.0 / math.sqrt(HD))
+            scores = jnp.exp(scores - jnp.max(scores, axis=1, keepdims=True))
+            probs = (scores / jnp.sum(scores, axis=1, keepdims=True)).astype(jnp.bfloat16)
+            attended.append(
+                jnp.dot(probs, value, preferred_element_type=jnp.float32).astype(jnp.bfloat16)
+            )
+        if iteration == 0:
+            end_gather(head_v, head_rows, head_send, head_recv)
+            folded_v[...] = jnp.dot(
+                out_v[...], head_v[...], preferred_element_type=jnp.float32
+            ).astype(jnp.bfloat16)
+            residual_table = jnp.dot(in_v[...], head_v[...], preferred_element_type=jnp.float32)
+            residual_high = residual_table.astype(jnp.bfloat16)
+            residual_low = (residual_table - residual_high.astype(jnp.float32)).astype(
+                jnp.bfloat16
+            )
+            residual_pair = jnp.concatenate([residual_high, residual_low], axis=0)
+        partial = jnp.dot(
+            jnp.concatenate(attended, axis=1), folded_v[...], preferred_element_type=jnp.float32
+        )
+        part_v[iteration] = partial.reshape(tensor_size, rows, channels)
+        for k in range(1, tensor_size):
+            target = lax.rem(mine + k, tensor_size)
+            copy = to_tensor(
+                part_v.at[iteration, target],
+                landed_v.at[iteration, k],
+                part_send.at[iteration, k],
+                part_recv.at[iteration, k],
+                target,
+            )
+            copy.start()
+            sends.append(copy)
+        own = own_v[...] if iteration == 0 else guess_v[iteration, mine]
+        velocity = jnp.dot(
+            jnp.concatenate([own, own], axis=1), residual_pair, preferred_element_type=jnp.float32
+        )
+        velocity = velocity + part_v[iteration, mine]
+        for k in range(1, tensor_size):
+            to_tensor(
+                part_v.at[iteration, mine],
+                landed_v.at[iteration, k],
+                part_send.at[iteration, k],
+                part_recv.at[iteration, k],
+                mine,
+            ).wait_recv()
+            velocity = velocity + landed_v[iteration, k]
+        drift = step_size * velocity
+        drift_v[iteration] = drift
+        for k in range(1, tm_size):
+            copy = to_tm(
+                drift_v.at[iteration],
+                drifts_v.at[iteration, k],
+                drift_send.at[iteration, k],
+                drift_recv.at[iteration, k],
+                lax.rem(me + k, tm_size),
+            )
+            copy.start()
+            sends.append(copy)
+        window = start_own
+        for k in range(1, tm_size):
+            to_tm(
+                drift_v.at[iteration],
+                drifts_v.at[iteration, k],
+                drift_send.at[iteration, k],
+                drift_recv.at[iteration, k],
+                me,
+            ).wait_recv()
+            reached = jnp.where(k <= me, 1.0, 0.0)
+            window = window + jnp.where(reached > 0.5, drifts_v[iteration, k], 0.0)
+        if iteration + 1 < ITERS:
+            guess_v[iteration + 1, mine] = window.astype(jnp.bfloat16)
+            later = iteration + 1
+            sends += share(guess_v.at[later], guess_send.at[later], guess_recv.at[later])
+            shared(guess_v.at[later], guess_send.at[later], guess_recv.at[later])
+        else:
+            o_ref[0] = window + drift
+    for copy in sends:
+        copy.wait_send()
+
+
+def fused(tm_size, tensor_size, *arrays):
+    start, _, _, in_w, mod_w, qkv_w, out_w, head_w = arrays
+    rows, channels = start.shape
+    bf16, f32 = jnp.bfloat16, jnp.float32
+    dma = pltpu.SemaphoreType.DMA
+    anywhere = pl.BlockSpec(memory_space=pl.ANY)
+    scalar = pl.BlockSpec(memory_space=pltpu.SMEM)
+    vector = pl.BlockSpec(memory_space=pltpu.VMEM)
+    return pl.pallas_call(
+        lambda *refs: fused_kernel(tm_size, tensor_size, *refs),
+        name="picard",
+        out_shape=jax.ShapeDtypeStruct((1, rows, channels), f32),
+        in_specs=[vector, scalar, scalar] + [anywhere] * 5,
+        out_specs=vector,
+        scratch_shapes=[
+            pltpu.VMEM(mod_w.shape, bf16),
+            pltpu.VMEM(qkv_w.shape, bf16),
+            pltpu.VMEM(out_w.shape, bf16),
+            pltpu.VMEM((channels, D), bf16),
+            pltpu.VMEM((D, channels), bf16),
+            pltpu.VMEM((tensor_size, 1, mod_w.shape[1]), f32),
+            pltpu.VMEM((channels, D), bf16),
+            pltpu.VMEM((channels + 16, D), bf16),
+            pltpu.VMEM((2 * channels, qkv_w.shape[1]), bf16),
+            pltpu.VMEM((1, qkv_w.shape[1]), f32),
+            pltpu.VMEM((out_w.shape[0], channels), bf16),
+            pltpu.VMEM((ITERS, tensor_size, rows, channels), bf16),
+            pltpu.VMEM((rows, channels), bf16),
+            pltpu.VMEM((ITERS, tensor_size, rows, channels), f32),
+            pltpu.VMEM((ITERS, tensor_size, rows, channels), f32),
+            pltpu.VMEM((ITERS, rows, channels), f32),
+            pltpu.VMEM((ITERS, tm_size, rows, channels), f32),
+            dma((5,)),
+            dma((tm_size,)),
+            dma((tm_size,)),
+            dma((tm_size,)),
+            dma((tm_size,)),
+            dma((tensor_size,)),
+            dma((tensor_size,)),
+            dma((ITERS, tensor_size)),
+            dma((ITERS, tensor_size)),
+            dma((ITERS, tensor_size)),
+            dma((ITERS, tensor_size)),
+            dma((ITERS, tm_size)),
+            dma((ITERS, tm_size)),
+        ],
+        compiler_params=pltpu.CompilerParams(
+            collective_id=0, has_side_effects=True, vmem_limit_bytes=48 * 1024 * 1024
+        ),
+    )(*arrays)
+
+
+def aligned(tm_size, tensor_size, arrays):
+    start, times, _, in_w, mod_w, qkv_w, out_w, head_w = arrays
+    return (
+        times.shape[0] == 1
+        and tm_size % 2 == 0
+        and in_w.shape[0] % 16 == 0
+        and head_w.shape[0] % 16 == 0
+        and start.shape[0] % 16 == 0
+        and mod_w.shape[1] % 128 == 0
+        and out_w.shape[0] % 128 == 0
+    )
+
+
+def device_program(tm_size, tensor_size):
+    def run(*arrays):
+        if aligned(tm_size, tensor_size, arrays):
+            return fused(tm_size, tensor_size, *arrays)
+        return local(*arrays)
+
+    return run
+
+
 def solution(mesh):
     return jax.shard_map(
-        local,
+        device_program(mesh.shape["tm"], mesh.shape["tensor"]),
         mesh=mesh,
         in_specs=(
             P(("groups", "tensor"), None),

time: 163 us -> 45.8 us (0.28)
  blocking collectives: 68.9 us -> 0 us
  Pallas kernels: 0 us -> 37.8 us
  waiting for transfers between devices: 36.8 us -> 0 us
  matrix products: 31.9 us -> 0 us
  between operations: 14.9 us -> 1.32 us
  other arithmetic: 3.61 us -> 0 us
    all_gather x7 -> x0, blocking collectives: 68.9 us -> none  [the longest x1 13.4 us: local(): start_all = lax.all_gather(start_latent, 'tensor', axis=0, tiled=True)]
    pallas_call x0 -> x1, Pallas kernels: none -> 37.8 us  [fused(): pl.pallas_call(lambda *refs: fused_kernel(tm_size, tensor_size, *refs), n...]
    reduce_scatter x2 -> x0, waiting for transfers between devices: 36.8 us -> none  [local(): lax.psum_scatter(stacked, 'tensor', scatter_dimension=1, tiled=True)]
    dot_general x14 -> x0, matrix products: 29.4 us -> none  [the longest x2 11.8 us: evaluate(): jnp.dot(normed, qkv_weight, preferred_element_type=jnp.float32)]
    unnamed x20 -> x11, local copies, waits for them, and re-layouts: 2.45 us -> 6.33 us
    convert_element_type x2 -> x0, local copies, waits for them, and re-layouts: 3.82 us -> none  [evaluate(): jnp.dot(normed, qkv_weight, preferred_element_type=jnp.float32)]
    sub x2 -> x0, matrix products: 2.54 us -> none  [one_block(): attention_weights = jax.nn.softmax(scores, axis=-1).astype(jnp.bfloat16)]
  transfers between devices with their start and end apart: 2 -> 0, of which waited for: 2 -> 0; matrix products, arithmetic and copies ran while one was open for 0% -> 0% of each run, Pallas kernels for 0% -> 0%
where the time goes in v1:
time: 45.8 us; the launch traced here: 45.5 us
  Pallas kernels  37.8 us (83%)
  local copies, waits for them, and re-layouts  6.33 us (14%)
  between operations  1.32 us (3%)
    pallas_call x1, Pallas kernels, fused(): pl.pallas_call(lambda *refs: fused_kernel(tm_size, tensor_size, *refs), n...  37.8 us
    unnamed x11, local copies, waits for them, and re-layouts  6.33 us

profile of v1, /device:TPU:0, one launch (start us, length us, event | category | flops | bytes accessed | tf_op | source)
XLA Modules:
  0.0 45.5 jit_solution(10573381011237274491)
XLA Ops:
  1.3 0.0 copy-start
  1.3 1.9 %copy-done = bf16[512,3072]{1,0:T(8,128)(2,1)S(1)} copy-done((bf16[512,3072]{1,0:T(8,128)(2,1)S(1)}, bf16[512,3072]{1,0:T(8,128)(2,1)}, u32[]{:S(2)}) %copy-start) | copy-done | bytes 3145752
  3.2 0.0 copy-start.1
  3.2 1.3 %copy-done.1 = bf16[256,2304]{1,0:T(8,128)(2,1)S(1)} copy-done((bf16[256,2304]{1,0:T(8,128)(2,1)S(1)}, bf16[256,2304]{1,0:T(8,128)(2,1)}, u32[]{:S(2)}) %copy-start.1) | copy-done | bytes 1179672
  4.5 0.0 copy-start.2
  4.5 0.9 %copy-done.2 = bf16[32,3072]{1,0:T(8,128)(2,1)S(1)} copy-done((bf16[32,3072]{1,0:T(8,128)(2,1)S(1)}, bf16[32,3072]{1,0:T(8,128)(2,1)}, u32[]{:S(2)}) %copy-start.2) | copy-done | bytes 196632
  5.4 0.0 copy-start.3
  5.4 0.9 %copy-done.3 = bf16[768,128]{1,0:T(8,128)(2,1)S(1)} copy-done((bf16[768,128]{1,0:T(8,128)(2,1)S(1)}, bf16[768,128]{1,0:T(8,128)(2,1)}, u32[]{:S(2)}) %copy-start.3) | copy-done | bytes 196632
  6.3 0.0 copy-start.4
  6.3 0.7 %copy-done.4 = f32[32,128]{1,0:T(8,128)S(1)} copy-done((f32[32,128]{1,0:T(8,128)S(1)}, f32[32,128]{1,0:T(8,128)}, u32[]{:S(2)}) %copy-start.4) | copy-done | bytes 16408
  7.0 37.8 %picard.1 = f32[1,32,128]{2,1,0:T(8,128)S(1)} custom-call(f32[32,128]{1,0:T(8,128)S(1)} %copy-done.4, s32[1]{0:T(128)S(6)} %copy.10.refs_1_, s32[1]{0:T(128)S(6)} %copy.11.refs_2_, bf16[32,3072]{1,0:T(8,128)(2,1)S(1)} %copy-done.2, bf16[256,2304]{1,0:T(8,128)(2,1)S(1)} %copy-done.1, bf16[3072,1536]{1,0:T(8,128)(2,1)} %refs_5_.1, ...), custom_call_target="tpu_custom_call" | custom-call | tf_op jit(solution)/shard_map/picard/pallas_call | solution.py:479
  44.9 0.6 %copy.12 = f32[1,32,128]{2,1,0:T(8,128)} copy(f32[1,32,128]{2,1,0:T(8,128)S(1)} %picard.1) | data formatting | bytes 32768
Async XLA Ops:
  1.3 1.9 %copy-start = (bf16[512,3072]{1,0:T(8,128)(2,1)S(1)}, bf16[512,3072]{1,0:T(8,128)(2,1)}, u32[]{:S(2)}) copy-start(bf16[512,3072]{1,0:T(8,128)(2,1)} %refs_6_.1) | copy-start | bytes 9437188
  3.2 1.3 %copy-start.1 = (bf16[256,2304]{1,0:T(8,128)(2,1)S(1)}, bf16[256,2304]{1,0:T(8,128)(2,1)}, u32[]{:S(2)}) copy-start(bf16[256,2304]{1,0:T(8,128)(2,1)} %refs_4_.1) | copy-start | bytes 3538948
  4.5 0.9 %copy-start.2 = (bf16[32,3072]{1,0:T(8,128)(2,1)S(1)}, bf16[32,3072]{1,0:T(8,128)(2,1)}, u32[]{:S(2)}) copy-start(bf16[32,3072]{1,0:T(8,128)(2,1)} %refs_3_.1) | copy-start | bytes 589828
  5.4 0.9 %copy-start.3 = (bf16[768,128]{1,0:T(8,128)(2,1)S(1)}, bf16[768,128]{1,0:T(8,128)(2,1)}, u32[]{:S(2)}) copy-start(bf16[768,128]{1,0:T(8,128)(2,1)} %refs_7_.1) | copy-start | bytes 589828
  6.3 0.7 %copy-start.4 = (f32[32,128]{1,0:T(8,128)S(1)}, f32[32,128]{1,0:T(8,128)}, u32[]{:S(2)}) copy-start(f32[32,128]{1,0:T(8,128)} %refs_0_.1) | copy-start | bytes 49156

commit v2 on v1

--- a/solution.py
+++ b/solution.py
@@ -172,8 +172,10 @@
     own_v,
     part_v,
     landed_v,
-    drift_v,
-    drifts_v,
+    whole_v,
+    start_v,
+    time_s,
+    step_s,
     local_sem,
     in_send,
     in_recv,
@@ -185,8 +187,6 @@
     guess_recv,
     part_send,
     part_recv,
-    drift_send,
-    drift_recv,
 ):
     me = lax.axis_index("tm")
     mine = lax.axis_index("tensor")
@@ -200,15 +200,15 @@
     heads = qkv_ref.shape[1] // (3 * HD)
 
     barrier = pltpu.get_barrier_semaphore()
-    for k in range(1, tm_size):
-        pl.semaphore_signal(
-            barrier, inc=1, device_id={"tm": lax.rem(me + k, tm_size)}, device_id_type=MESH
-        )
-    for k in range(1, tensor_size):
+    peers = [(a, b) for a in range(tm_size) for b in range(tensor_size)][1:]
+    for a, b in peers:
         pl.semaphore_signal(
             barrier,
             inc=1,
-            device_id={"tensor": lax.rem(mine + k, tensor_size)},
+            device_id={
+                "tm": lax.rem(me + a, tm_size),
+                "tensor": lax.rem(mine + b, tensor_size),
+            },
             device_id_type=MESH,
         )
 
@@ -220,9 +220,12 @@
     copy_head = pltpu.make_async_copy(head_ref, row_block(head_v, me, head_rows), local_sem.at[2])
     copy_out = pltpu.make_async_copy(out_w_ref, out_v, local_sem.at[3])
     copy_qkv = pltpu.make_async_copy(qkv_ref, qkv_v, local_sem.at[4])
-    for copy in (copy_mod, copy_in, copy_head, copy_out, copy_qkv):
+    copy_start = pltpu.make_async_copy(start_ref, start_v, local_sem.at[5])
+    copy_time = pltpu.make_async_copy(time_ref, time_s, local_sem.at[6])
+    copy_step = pltpu.make_async_copy(step_ref, step_s, local_sem.at[7])
+    for copy in (copy_time, copy_step, copy_start, copy_mod, copy_in, copy_head, copy_out, copy_qkv):
         copy.start()
-    pl.semaphore_wait(barrier, tm_size - 1 + tensor_size - 1)
+    pl.semaphore_wait(barrier, len(peers))
 
     def to_tm(src, dst, send, recv, target):
         return pltpu.make_async_remote_copy(
@@ -297,7 +300,8 @@
     sends += start_gather(in_ref, in_v, in_rows, in_send, in_recv)
     sends += start_gather(head_ref, head_v, head_rows, head_send, head_recv)
 
-    start_own = start_ref[...]
+    copy_start.wait()
+    start_own = start_v[...]
     own_v[...] = start_own.astype(jnp.bfloat16)
     guess_v[0, mine] = start_own.astype(jnp.bfloat16)
     sends += share(guess_v.at[0], guess_send.at[0], guess_recv.at[0])
@@ -305,7 +309,8 @@
     half = mod_ref.shape[0] // 2
     order = lax.broadcasted_iota(jnp.int32, (8, half), 1).astype(jnp.float32)
     frequency = jnp.exp(-math.log(10000.0) * order / half)
-    angles = time_ref[0].astype(jnp.float32) * frequency
+    copy_time.wait()
+    angles = time_s[0].astype(jnp.float32) * frequency
     embedding = jnp.concatenate([jnp.cos(angles), jnp.sin(angles)], axis=1).astype(jnp.bfloat16)
     copy_mod.wait()
     mod_part = jnp.dot(embedding, mod_v[...], preferred_element_type=jnp.float32)
@@ -343,17 +348,6 @@
         centered_v[r : r + 32] = block.astype(jnp.bfloat16)
         scaled_v[r : r + 32] = (block * scales).astype(jnp.bfloat16)
 
-    copy_qkv.wait()
-    for h in range(heads):
-        columns = slice(3 * HD * h, 3 * HD * (h + 1))
-        product = jnp.dot(
-            scaled_v[...], qkv_v[:, columns], preferred_element_type=jnp.float32
-        )
-        main = product[:channels]
-        main_high = main.astype(jnp.bfloat16)
-        table_v[:channels, columns] = main_high
-        table_v[channels:, columns] = (main - main_high.astype(jnp.float32)).astype(jnp.bfloat16)
-        shift_v[:, columns] = product[channels : channels + 1] + product[channels + 1 : channels + 2]
     centered = centered_v[...]
     spread_table = lax.dot_general(
         centered, centered, (((1,), (1,)), ((), ())), preferred_element_type=jnp.float32
@@ -362,11 +356,24 @@
     spread_low = (spread_table - spread_high.astype(jnp.float32)).astype(jnp.bfloat16)
     spread_pair = jnp.concatenate([spread_high, spread_low], axis=0)
 
-    sends += relay_gather(head_v, head_rows, head_send, head_recv)
+    copy_qkv.wait()
+    for h in range(heads):
+        if h == heads - 1:
+            sends += relay_gather(head_v, head_rows, head_send, head_recv)
+        columns = slice(3 * HD * h, 3 * HD * (h + 1))
+        product = jnp.dot(
+            scaled_v[...], qkv_v[:, columns], preferred_element_type=jnp.float32
+        )
+        main = product[:channels]
+        main_high = main.astype(jnp.bfloat16)
+        table_v[:channels, columns] = main_high
+        table_v[channels:, columns] = (main - main_high.astype(jnp.float32)).astype(jnp.bfloat16)
+        shift_v[:, columns] = product[channels : channels + 1] + product[channels + 1 : channels + 2]
     copy_head.wait()
     shared(guess_v.at[0], guess_send.at[0], guess_recv.at[0])
 
-    step_size = step_ref[0].astype(jnp.float32) / STEP_DIVISOR
+    copy_step.wait()
+    step_size = step_s[0].astype(jnp.float32) / STEP_DIVISOR
     residual_pair = None
     for iteration in range(ITERS):
         guess = jnp.concatenate([guess_v[iteration, k] for k in range(tensor_size)], axis=0)
@@ -399,64 +406,50 @@
             folded_v[...] = jnp.dot(
                 out_v[...], head_v[...], preferred_element_type=jnp.float32
             ).astype(jnp.bfloat16)
+        partial = jnp.dot(
+            jnp.concatenate(attended, axis=1), folded_v[...], preferred_element_type=jnp.float32
+        )
+        if iteration == 0:
             residual_table = jnp.dot(in_v[...], head_v[...], preferred_element_type=jnp.float32)
             residual_high = residual_table.astype(jnp.bfloat16)
             residual_low = (residual_table - residual_high.astype(jnp.float32)).astype(
                 jnp.bfloat16
             )
             residual_pair = jnp.concatenate([residual_high, residual_low], axis=0)
-        partial = jnp.dot(
-            jnp.concatenate(attended, axis=1), folded_v[...], preferred_element_type=jnp.float32
-        )
-        part_v[iteration] = partial.reshape(tensor_size, rows, channels)
-        for k in range(1, tensor_size):
-            target = lax.rem(mine + k, tensor_size)
-            copy = to_tensor(
-                part_v.at[iteration, target],
-                landed_v.at[iteration, k],
-                part_send.at[iteration, k],
-                part_recv.at[iteration, k],
-                target,
+        own = own_v[...] if iteration == 0 else guess_v[iteration, mine]
+        residual = jnp.dot(
+            jnp.concatenate([own, own], axis=1), residual_pair, preferred_element_type=jnp.float32
+        )
+        partial = (step_size * partial).reshape(tensor_size, rows, channels)
+        whole_v[...] = partial
+        part_v[iteration] = partial.astype(jnp.bfloat16)
+        drift = whole_v[mine] + step_size * residual
+        part_v[iteration, mine] = drift.astype(jnp.bfloat16)
+
+        def exchange(a, b):
+            there = lax.rem(mine + b, tensor_size)
+            slot = a * tensor_size + b
+            return pltpu.make_async_remote_copy(
+                src_ref=part_v.at[iteration, there],
+                dst_ref=landed_v.at[iteration, slot],
+                send_sem=part_send.at[iteration, slot],
+                recv_sem=part_recv.at[iteration, slot],
+                device_id={"tm": lax.rem(me + a, tm_size), "tensor": there},
+                device_id_type=MESH,
             )
-            copy.start()
-            sends.append(copy)
-        own = own_v[...] if iteration == 0 else guess_v[iteration, mine]
-        velocity = jnp.dot(
-            jnp.concatenate([own, own], axis=1), residual_pair, preferred_element_type=jnp.float32
-        )
-        velocity = velocity + part_v[iteration, mine]
-        for k in range(1, tensor_size):
-            to_tensor(
-                part_v.at[iteration, mine],
-                landed_v.at[iteration, k],
-                part_send.at[iteration, k],
-                part_recv.at[iteration, k],
-                mine,
-            ).wait_recv()
-            velocity = velocity + landed_v[iteration, k]
-        drift = step_size * velocity
-        drift_v[iteration] = drift
-        for k in range(1, tm_size):
-            copy = to_tm(
-                drift_v.at[iteration],
-                drifts_v.at[iteration, k],
-                drift_send.at[iteration, k],
-                drift_recv.at[iteration, k],
-                lax.rem(me + k, tm_size),
-            )
+
+        for a, b in peers[::-1]:
+            copy = exchange(a, b)
             copy.start()
             sends.append(copy)
         window = start_own
-        for k in range(1, tm_size):
-            to_tm(
-                drift_v.at[iteration],
-                drifts_v.at[iteration, k],
-                drift_send.at[iteration, k],
-                drift_recv.at[iteration, k],
-                me,
-            ).wait_recv()
-            reached = jnp.where(k <= me, 1.0, 0.0)
-            window = window + jnp.where(reached > 0.5, drifts_v[iteration, k], 0.0)
+        for a, b in peers:
+            exchange(a, b).wait_recv()
+            arrived = landed_v[iteration, a * tensor_size + b].astype(jnp.float32)
+            if a == 0:
+                drift = drift + arrived
+            else:
+                window = window + jnp.where(a <= me, 1.0, 0.0) * arrived
         if iteration + 1 < ITERS:
             guess_v[iteration + 1, mine] = window.astype(jnp.bfloat16)
             later = iteration + 1
@@ -474,13 +467,12 @@
     bf16, f32 = jnp.bfloat16, jnp.float32
     dma = pltpu.SemaphoreType.DMA
     anywhere = pl.BlockSpec(memory_space=pl.ANY)
-    scalar = pl.BlockSpec(memory_space=pltpu.SMEM)
     vector = pl.BlockSpec(memory_space=pltpu.VMEM)
     return pl.pallas_call(
         lambda *refs: fused_kernel(tm_size, tensor_size, *refs),
         name="picard",
         out_shape=jax.ShapeDtypeStruct((1, rows, channels), f32),
-        in_specs=[vector, scalar, scalar] + [anywhere] * 5,
+        in_specs=[anywhere] * 8,
         out_specs=vector,
         scratch_shapes=[
             pltpu.VMEM(mod_w.shape, bf16),
@@ -496,11 +488,13 @@
             pltpu.VMEM((out_w.shape[0], channels), bf16),
             pltpu.VMEM((ITERS, tensor_size, rows, channels), bf16),
             pltpu.VMEM((rows, channels), bf16),
-            pltpu.VMEM((ITERS, tensor_size, rows, channels), f32),
-            pltpu.VMEM((ITERS, tensor_size, rows, channels), f32),
-            pltpu.VMEM((ITERS, rows, channels), f32),
-            pltpu.VMEM((ITERS, tm_size, rows, channels), f32),
-            dma((5,)),
+            pltpu.VMEM((ITERS, tensor_size, rows, channels), bf16),
+            pltpu.VMEM((ITERS, tm_size * tensor_size, rows, channels), bf16),
+            pltpu.VMEM((tensor_size, rows, channels), f32),
+            pltpu.VMEM((rows, channels), f32),
+            pltpu.SMEM((1,), jnp.int32),
+            pltpu.SMEM((1,), jnp.int32),
+            dma((8,)),
             dma((tm_size,)),
             dma((tm_size,)),
             dma((tm_size,)),
@@ -509,13 +503,11 @@
             dma((tensor_size,)),
             dma((ITERS, tensor_size)),
             dma((ITERS, tensor_size)),
-            dma((ITERS, tensor_size)),
-            dma((ITERS, tensor_size)),
-            dma((ITERS, tm_size)),
-            dma((ITERS, tm_size)),
+            dma((ITERS, tm_size * tensor_size)),
+            dma((ITERS, tm_size * tensor_size)),
         ],
         compiler_params=pltpu.CompilerParams(
-            collective_id=0, has_side_effects=True, vmem_limit_bytes=48 * 1024 * 1024
+            collective_id=0, has_side_effects=True, vmem_limit_bytes=67043328
         ),
     )(*arrays)
 

time: 45.8 us -> 39.8 us (0.87)
  local copies, waits for them, and re-layouts: 6.33 us -> 1.32 us
  Pallas kernels: 37.8 us -> 36.9 us
    unnamed x11 -> x1, local copies, waits for them, and re-layouts: 6.33 us -> 1.32 us
    pallas_call x1, Pallas kernels: 37.8 us -> 36.9 us  [fused(): pl.pallas_call(lambda *refs: fused_kernel(tm_size, tensor_size, *refs), n...]
where the time goes in v2:
time: 39.8 us; the launch traced here: 39.6 us
  Pallas kernels  36.9 us (93%)
  local copies, waits for them, and re-layouts  1.32 us (3%)
  between operations  1.3 us (3%)
    pallas_call x1, Pallas kernels, fused(): pl.pallas_call(lambda *refs: fused_kernel(tm_size, tensor_size, *refs), n...  36.9 us
    unnamed x1, local copies, waits for them, and re-layouts  1.32 us

profile of v2, /device:TPU:0, one launch (start us, length us, event | category | flops | bytes accessed | tf_op | source)
XLA Modules:
  0.0 39.6 jit_solution(11418437787675041992)
XLA Ops:
  1.3 36.9 %picard.1 = f32[1,32,128]{2,1,0:T(8,128)} custom-call(f32[32,128]{1,0:T(8,128)} %refs_0_.1, s32[1]{0:T(128)S(6)} %copy.10.refs_1_, s32[1]{0:T(128)S(6)} %copy.11.refs_2_, bf16[32,3072]{1,0:T(8,128)(2,1)} %refs_3_.1, bf16[256,2304]{1,0:T(8,128)(2,1)} %refs_4_.1, bf16[3072,1536]{1,0:T(8,128)(2,1)} %refs_5_.1, bf16[512,3072]{1,0:T(8,128)(2,1)} %refs_6_.1, ...), custom_call_target="tpu_custom_call" | custom-call | tf_op jit(solution)/shard_map/picard/pallas_call | solution.py:471
  38.2 1.3 %copy.12 = f32[1,32,128]{2,1,0:T(8,128)} copy(f32[1,32,128]{2,1,0:T(8,128)} %picard.1) | data formatting | bytes 32768
